TPU v7x, 32 devices: a whole 2x2x4 slice. The times are simulated.
32 devices in a mesh: dp: 8 (over y, x, core), tensor: 4 (over z).
Axes of the slice: x: 2, y: 2, z: 4, core: 2. Of those that a mesh axis runs over, the one named last changes fastest.
Arguments:
- hidden: bfloat16 [16384, 768], P('dp'), may hold values from -6 to 6
- teacher: float32 [16384, 768], P('dp'), may hold values from -6 to 6
- valid: int32 [8, 2048], P('dp'), may hold values from 0 to 1, as said below
- w_qkv: bfloat16 [3, 768, 768], P(None, None, 'tensor'), may hold values from -0.21875 to 0.21875
- b_qv: float32 [2, 768], P(None, 'tensor'), may hold values from -1 to 1
- w_attn_out: bfloat16 [768, 768], P('tensor'), may hold values from -1.25 to 1.25
- b_attn_out: float32 [768], replicated, may hold values from -1.5 to 1.5
- gain_one: float32 [768], replicated, may hold values from 0.5 to 1.5
- bias_one: float32 [768], replicated, may hold values from -1.5 to 1.5
- w_up: bfloat16 [768, 3072], P(None, 'tensor'), may hold values from -0.21875 to 0.21875
- b_up: float32 [3072], P('tensor'), may hold values from -2.5 to 2.5
- w_down: bfloat16 [3072, 768], P('tensor'), may hold values from -0.109375 to 0.109375
- b_down: float32 [768], replicated, may hold values from -1.5 to 1.5
- gain_two: float32 [768], replicated, may hold values from 0.5 to 1.5
- bias_two: float32 [768], replicated, may hold values from -1.5 to 1.5
- pairwise_gate_odds_table: float32 [12, 512, 512], P('tensor'), may hold values from -5 to 5
- gate_random_perturbation: float32 [12, 512, 512], P('tensor'), may hold values from -2 to 2
Outputs:
- out_states: float32 [16384, 768], P('dp')
- loss: float32 [], replicated
- grad_hidden: float32 [16384, 768], P('dp')
- grad_w_qkv: float32 [3, 768, 768], P(None, None, 'tensor')
- grad_b_qv: float32 [2, 768], P(None, 'tensor')
- grad_w_attn_out: float32 [768, 768], P('tensor')
- grad_b_attn_out: float32 [768], replicated
- grad_gain_one: float32 [768], replicated
- derivative_first_offset: float32 [768], replicated
- grad_w_up: float32 [768, 3072], P(None, 'tensor')
- grad_b_up: float32 [3072], P('tensor')
- grad_w_down: float32 [3072, 768], P('tensor')
- grad_b_down: float32 [768], replicated
- grad_gain_two: float32 [768], replicated
- grad_bias_two: float32 [768], replicated
- grad_mask_logits: float32 [12, 512, 512], P('tensor')
Inputs may be any that keep to these rules, and one draw needn't show every extreme that they name: The first token of every sequence is valid.
All inputs are finite; a program needn't handle non-finite values.
Results may differ from a plain program's by a relative error of at most 0.019.
Values may be sent and summed in bfloat16 or wider, within the bound.
No kernel may reach another device: no remote copies, remote signals or barrier semaphores. Data moves between devices by JAX's collectives and lax.ppermute only.
A program may use at most 256 MiB of HBM per device.

v0:
```python
import math
import jax
import jax.numpy as jnp
from jax import lax
from jax.sharding import PartitionSpec as P

BLOCK = 256
epsilon = 1e-06
gumbel_softening_factor = 0.5


def normed(resid, gain, shift):
    average = jnp.mean(resid, axis=-1, keepdims=True)
    centred = resid - average
    variance = jnp.mean(centred * centred, axis=-1, keepdims=True)
    return centred * lax.rsqrt(variance + epsilon) * gain + shift


def exact_gelu(inputs):
    return jax.nn.gelu(inputs, approximate=False)


def block_scores(queries, key_vectors, gate_natural_log, block_index, score_scale):
    period = gate_natural_log.shape[1]
    head_count = gate_natural_log.shape[0]
    head_width = queries.shape[1] // head_count
    key_span = (block_index + 1) * period
    query_rows = queries[block_index * period : key_span].reshape(period, head_count, head_width)
    key_row_block = key_vectors[:key_span].reshape(key_span, head_count, head_width)
    scores = (
        jnp.einsum("qhd,khd->hqk", query_rows, key_row_block, preferred_element_type=jnp.float32)
        * score_scale
    )
    scores = scores + jnp.tile(gate_natural_log, (1, 1, block_index + 1))
    row_pos = lax.broadcasted_iota(jnp.int32, (period, key_span), 0) + block_index * period
    col_pos = lax.broadcasted_iota(jnp.int32, (period, key_span), 1)
    allowed = col_pos // BLOCK <= row_pos // BLOCK
    return jnp.where(allowed[None], scores, -1e30)


def body(
    hidden,
    teacher,
    valid,
    w_qkv,
    b_qv,
    w_attn_out,
    b_attn_out,
    gain_one,
    bias_one,
    w_up,
    b_up,
    w_down,
    b_down,
    gain_two,
    bias_two,
    pairwise_gate_odds_table,
    gate_random_perturbation,
):
    seq_tokens = hidden.shape[0]
    model_width = hidden.shape[1]
    period = pairwise_gate_odds_table.shape[1]
    head_count = pairwise_gate_odds_table.shape[0]
    local_width = w_qkv.shape[2]
    head_width = local_width // head_count
    score_scale = 1.0 / math.sqrt(head_width)
    num_blocks = seq_tokens // period
    projected = jnp.einsum("td,kde->kte", hidden, w_qkv, preferred_element_type=jnp.float32)
    queries = (projected[0] + b_qv[0]).astype(jnp.bfloat16)
    key_vectors = projected[1].astype(jnp.bfloat16)
    values = (projected[2] + b_qv[1]).astype(jnp.bfloat16)

    def soft_mask(affinity_preactivations):
        return jax.nn.log_sigmoid(
            (affinity_preactivations + gate_random_perturbation) / gumbel_softening_factor
        )

    gate_natural_log, mask_pull = jax.vjp(soft_mask, pairwise_gate_odds_table)
    contexts = []
    logarithm_sums = []
    for block_index in range(num_blocks):
        scores = block_scores(queries, key_vectors, gate_natural_log, block_index, score_scale)
        highest = jnp.max(scores, axis=-1, keepdims=True)
        exponent = jnp.exp(scores - highest)
        totals = jnp.sum(exponent, axis=-1, keepdims=True)
        soft_weights = (exponent / totals).astype(jnp.bfloat16)
        logarithm_sums.append(highest + jnp.log(totals))
        key_span = (block_index + 1) * period
        value_rows = values[:key_span].reshape(key_span, head_count, head_width)
        contexts.append(
            jnp.einsum("hqk,khd->qhd", soft_weights, value_rows, preferred_element_type=jnp.float32)
        )
    context = (
        jnp.concatenate(contexts, axis=0).reshape(seq_tokens, local_width).astype(jnp.bfloat16)
    )
    hidden_wide = hidden.astype(jnp.float32)
    attn_part = jnp.dot(context, w_attn_out, preferred_element_type=jnp.float32)
    attention = lax.psum(attn_part.astype(jnp.bfloat16), "tensor").astype(jnp.float32) + b_attn_out
    first, first_pull = jax.vjp(normed, hidden_wide + attention, gain_one, bias_one)
    first_low = first.astype(jnp.bfloat16)
    before = jnp.dot(first_low, w_up, preferred_element_type=jnp.float32) + b_up
    activated, gelu_pull = jax.vjp(exact_gelu, before)
    act_low = activated.astype(jnp.bfloat16)
    ffn_part = jnp.dot(act_low, w_down, preferred_element_type=jnp.float32)
    feedforward = lax.psum(ffn_part.astype(jnp.bfloat16), "tensor").astype(jnp.float32) + b_down
    out_states, second_pull = jax.vjp(normed, first + feedforward, gain_two, bias_two)
    valid_rows = valid[0].astype(jnp.float32)[:, None]
    residue = out_states - teacher
    local_error = jnp.sum(valid_rows * residue * residue)
    local_count = jnp.sum(valid_rows)
    total_valid, total_error = lax.psum((local_count, local_error), "dp")
    loss_value = total_error / (total_valid * model_width)
    factor = seq_tokens / total_valid
    upstream_derivative = 2.0 * factor * valid_rows * residue
    grad_second, grad_gain_two, grad_bias_two = second_pull(upstream_derivative)
    grad_ffn = grad_second.astype(jnp.bfloat16)
    grad_b_down = jnp.sum(grad_ffn, axis=0, dtype=jnp.float32)
    grad_w_down = jnp.einsum("tf,td->fd", act_low, grad_ffn, preferred_element_type=jnp.float32)
    grad_act = jnp.einsum("td,fd->tf", grad_ffn, w_down, preferred_element_type=jnp.float32)
    grad_before = gelu_pull(grad_act)[0].astype(jnp.bfloat16)
    grad_b_up = jnp.sum(grad_before, axis=0, dtype=jnp.float32)
    grad_w_up = jnp.einsum("td,tf->df", first_low, grad_before, preferred_element_type=jnp.float32)
    back_first = jnp.einsum("tf,df->td", grad_before, w_up, preferred_element_type=jnp.float32)
    grad_first = grad_second + lax.psum(back_first.astype(jnp.bfloat16), "tensor").astype(
        jnp.float32
    )
    grad_resid, grad_gain_one, derivative_first_offset = first_pull(grad_first)
    grad_attn = grad_resid.astype(jnp.bfloat16)
    grad_b_attn_out = jnp.sum(grad_attn, axis=0, dtype=jnp.float32)
    grad_w_attn_out = jnp.einsum(
        "tc,td->cd", context, grad_attn, preferred_element_type=jnp.float32
    )
    grad_context = jnp.einsum(
        "td,cd->tc", grad_attn, w_attn_out, preferred_element_type=jnp.float32
    ).astype(jnp.bfloat16)
    grad_queries = []
    grad_keys = jnp.zeros((seq_tokens, head_count, head_width), jnp.float32)
    grad_values = jnp.zeros((seq_tokens, head_count, head_width), jnp.float32)
    grad_log_mask = jnp.zeros(gate_natural_log.shape, jnp.float32)
    for block_index in range(num_blocks):
        scores = block_scores(queries, key_vectors, gate_natural_log, block_index, score_scale)
        soft = jnp.exp(scores - logarithm_sums[block_index])
        start_row = block_index * period
        key_span = start_row + period
        grad_rows = grad_context[start_row:key_span].reshape(period, head_count, head_width)
        query_rows = queries[start_row:key_span].reshape(period, head_count, head_width)
        key_row_block = key_vectors[:key_span].reshape(key_span, head_count, head_width)
        value_rows = values[:key_span].reshape(key_span, head_count, head_width)
        grad_soft = jnp.einsum(
            "qhd,khd->hqk", grad_rows, value_rows, preferred_element_type=jnp.float32
        )
        inner = jnp.sum(soft * grad_soft, axis=-1, keepdims=True)
        grad_scores = (soft * (grad_soft - inner)).astype(jnp.bfloat16)
        grad_log_mask = grad_log_mask + jnp.sum(
            grad_scores.reshape(head_count, period, block_index + 1, period),
            axis=2,
            dtype=jnp.float32,
        )
        grad_queries.append(
            jnp.einsum(
                "hqk,khd->qhd", grad_scores, key_row_block, preferred_element_type=jnp.float32
            )
            * score_scale
        )
        grad_keys = grad_keys.at[:key_span].add(
            jnp.einsum("hqk,qhd->khd", grad_scores, query_rows, preferred_element_type=jnp.float32)
            * score_scale
        )
        grad_values = grad_values.at[:key_span].add(
            jnp.einsum(
                "hqk,qhd->khd",
                soft.astype(jnp.bfloat16),
                grad_rows,
                preferred_element_type=jnp.float32,
            )
        )
    grad_qkv = jnp.stack(
        [
            jnp.concatenate(grad_queries, axis=0).reshape(seq_tokens, local_width),
            grad_keys.reshape(seq_tokens, local_width),
            grad_values.reshape(seq_tokens, local_width),
        ]
    ).astype(jnp.bfloat16)
    grad_w_qkv = jnp.einsum("td,kte->kde", hidden, grad_qkv, preferred_element_type=jnp.float32)
    grad_b_qv = jnp.sum(grad_qkv[0::2], axis=1, dtype=jnp.float32)
    back_hidden = jnp.einsum("kte,kde->td", grad_qkv, w_qkv, preferred_element_type=jnp.float32)
    grad_hidden = grad_resid + lax.psum(back_hidden.astype(jnp.bfloat16), "tensor").astype(
        jnp.float32
    )
    mask_gradient = mask_pull(grad_log_mask)[0]
    summed = lax.psum(
        (
            grad_w_qkv,
            grad_b_qv,
            grad_w_attn_out,
            grad_b_attn_out,
            grad_gain_one,
            derivative_first_offset,
            grad_w_up,
            grad_b_up,
            grad_w_down,
            grad_b_down,
            grad_gain_two,
            grad_bias_two,
            mask_gradient,
        ),
        "dp",
    )
    return (
        out_states,
        loss_value,
        grad_hidden,
        summed[0],
        summed[1],
        summed[2],
        summed[3],
        summed[4],
        summed[5],
        summed[6],
        summed[7],
        summed[8],
        summed[9],
        summed[10],
        summed[11],
        summed[12],
    )


def solution(mesh):
    placed = (
        P("dp", None),
        P("dp", None),
        P("dp", None),
        P(None, None, "tensor"),
        P(None, "tensor"),
        P("tensor", None),
        P(),
        P(),
        P(),
        P(None, "tensor"),
        P("tensor"),
        P("tensor", None),
        P(),
        P(),
        P(),
        P("tensor", None, None),
        P("tensor", None, None),
    )
    return jax.shard_map(
        body,
        mesh=mesh,
        in_specs=placed,
        out_specs=(
            P("dp", None),
            P(),
            P("dp", None),
            P(None, None, "tensor"),
            P(None, "tensor"),
            P("tensor", None),
            P(),
            P(),
            P(),
            P(None, "tensor"),
            P("tensor"),
            P("tensor", None),
            P(),
            P(),
            P(),
            P("tensor", None, None),
        ),
        check_vma=False,
    )
```

profile of v0, /device:TPU:0, one launch (start us, length us, event | category | flops | bytes accessed | tf_op | source)
XLA Modules:
  0.0 1031.9 jit_solution(5200982813277051562)
XLA Ops:
  15.1 4.2 convolution_bitcast_fusion
  26.7 3.5 copy.54
  30.2 3.6 copy.55
  33.8 6.4 fusion.35
  40.2 3.6 copy.57
  46.0 7.0 tile.14
  53.0 9.6 copy.58
  62.6 6.6 tile.12
  69.1 9.2 tile.13
  78.3 7.7 tile.16
  86.1 15.9 %tile.17 = f32[3,512,2048]{2,1,0:T(8,128)} reshape(f32[3,512,4,512]{3,2,1,0:T(4,128)} %tile.16) | data formatting | bytes 25165824 | tf_op jit(solution)/shard_map/tile | solution.py:34
  126.1 6.7 fusion.143
  137.5 3.2 fusion.97
  144.6 123.8 %all-reduce.10.cloned.1.call-done = bf16[2048,768]{1,0:T(8,128)(2,1)} async-done(((bf16[2048,768]{1,0:T(8,128)(2,1)}), bf16[2048,768]{1,0:T(8,128)(2,1)}) %all-reduce.10.cloned.1.call-update) | async-done | bytes 3145744 | tf_op jit(solution)/shard_map/psum | solution.py:98
  268.4 4.1 fusion.17
  274.9 18.6 %multiply_convert_fusion.3 = (bf16[2048,768]{1,0:T(8,128)(2,1)S(1)}, f32[2048,768]{1,0:T(8,128)}, f32[2048,768]{1,0:T(8,128)}) fusion(f32[768]{0:T(1024)S(1)} %copy-done.118, bf16[768,768]{1,0:T(8,128)(2,1)S(1)} %copy-done, f32[768]{0:T(1024)S(1)} %copy-done.107, f32[768]{0:T(1024)S(1)} %copy-done.75, f32[2048]{0:T(1024)S(1)} %fusion.112, ...), kind=kOutput, calls=%fused_computation.44 | convolution fusion | flops 2533883904 | bytes 23228416 | tf_op jit(solution)/shard_map/dot_general | solution.py:101
  295.3 4.0 convolution_convert_fusion.1
  300.0 14.6 %psum.136 = f32[]{:T(128)} all-reduce(f32[]{:T(128)} %convert_reduce_fusion.4), channel_id=1, replica_groups=mesh['dp'=8,'tensor'=4] {'dp'}, use_global_device_ids=true, to_apply=%region_17.18 | all-reduce | flops 1 | bytes 8 | tf_op jit(solution)/shard_map/psum | solution.py:111
  315.3 104.2 %all-reduce.12.cloned.1.call-done = bf16[2048,768]{1,0:T(8,128)(2,1)} async-done(((bf16[2048,768]{1,0:T(8,128)(2,1)}), bf16[2048,768]{1,0:T(8,128)(2,1)}) %all-reduce.12.cloned.1.call-update) | async-done | bytes 3145744 | tf_op jit(solution)/shard_map/psum | solution.py:105
  419.5 5.2 fusion.138
  425.7 8.2 multiply_reduce_fusion.2
  433.9 3.4 fusion.137
  439.4 8.4 convert_reduce_fusion.1
  449.6 4.0 convolution_convert_fusion
  454.4 119.4 %all-reduce.14.cloned.1.call-done = bf16[2048,768]{1,0:T(8,128)(2,1)} async-done(((bf16[2048,768]{1,0:T(8,128)(2,1)}), bf16[2048,768]{1,0:T(8,128)(2,1)}) %all-reduce.14.cloned.1.call-update) | async-done | bytes 3145744 | tf_op jit(solution)/shard_map/psum | solution.py:124
  573.8 10.1 multiply_reduce_fusion.3
  583.9 6.0 fusion.136
  606.3 9.1 reshape.827
  615.5 5.2 multiply_reduce_fusion.1
  627.5 7.4 copy.64
  634.9 10.8 %multiply_reduce_fusion = (f32[3,512]{1,0:T(4,128)S(1)}, f32[3,512,2048]{2,1,0:T(8,128)}) fusion(f32[3,512,2048]{2,1,0:T(8,128)} %copy-done.2, f32[3,512]{1,0:T(4,128)S(1)} %log_add_fusion, bf16[512,3,64]{0,2,1:T(8,128)(2,1)S(1)} %bitcast.203, f32[2048,3,64]{0,2,1:T(8,128)S(1)} %bitcast.187, f32[3,64]{1,0:T(4,128)S(1)} %copy-done.74), kind=kOutput, calls=%fused_computation.1 | convolution fusion | flops 412875264 | bytes 26948352 | tf_op jit(solution)/shard_map/qhd,khd->hqk/dot_general | solution.py:149
  647.6 6.3 multiply_convert_fusion
  659.3 15.4 %reshape.829 = f32[3,512,4,512]{3,2,1,0:T(4,128)} reshape(bf16[3,512,2048]{2,1,0:T(8,128)(2,1)} %copy-done.5) | data formatting | bytes 18874368 | tf_op jit(solution)/shard_map/convert_element_type | solution.py:154
  674.7 11.9 %reduce_sum.323 = f32[3,512,512]{2,1,0:T(8,128)} reduce(f32[3,512,2,512]{3,2,1,0:T(2,128)} %reshape.827, f32[]{:T(128)} %constant.386.clone.1), dimensions={2}, to_apply=%region_48.49 | reduce | flops 786432 | bytes 9437188 | tf_op jit(solution)/shard_map/reduce_sum | solution.py:154
  686.6 3.5 copy.63
  690.1 7.0 reduce_sum.324
  697.1 12.7 %reduce_sum.325 = f32[3,512,512]{2,1,0:T(8,128)} reduce(f32[3,512,4,512]{3,2,1,0:T(4,128)} %reshape.829, f32[]{:T(128)} %constant.386.clone.1), dimensions={2}, to_apply=%region_50.51 | reduce | flops 2359296 | bytes 15728644 | tf_op jit(solution)/shard_map/reduce_sum | solution.py:154
  709.8 3.7 copy.65
  713.5 11.1 %fusion.30 = (f32[3,512,512]{1,2,0:T(8,128)}, bf16[3,512,512]{1,2,0:T(8,128)(2,1)S(1)}) fusion(f32[3,512,512]{1,2,0:T(8,128)} %copy.65, f32[3,512,512]{1,2,0:T(8,128)} %reduce_sum.324, f32[3,512,512]{1,2,0:T(8,128)} %copy.63, f32[3,512,512]{1,2,0:T(8,128)} %copy.54, f32[3,512,512]{1,2,0:T(8,128)} %copy.55, f32[3,512,512]{1,2,0:T(8,128)} %get-tuple-element.244, ...), kind=kLoop, calls=%fused_computation.86 | loop fusion | flops 20447232 | bytes 26750976 | tf_op jit(solution)/shard_map/transpose(jvp())/div | solution.py:75
  737.3 4.1 bitcast_convert_fusion
  741.8 7.1 fusion.148
  748.9 4.8 fusion.129
  755.4 3.2 fusion.70
  760.0 26.0 %all-reduce.2 = (f32[]{:T(128)}, f32[2,192]{1,0:T(2,128)}, f32[768]{0:T(1024)}, f32[768]{0:T(1024)}, f32[768]{0:T(1024)}, /*index=5*/f32[768]{0:T(1024)}, f32[768]{0:T(1024)}, f32[768]{0:T(1024)}, f32[768]{0:T(1024)}) all-reduce(f32[]{:T(128)} %get-tuple-element.182, ...), channel_id=1, replica_groups=mesh['dp'=8,'tensor'=4] {'dp'}, use_global_device_ids=true, to_apply=%region_15.16 | all-reduce | flops 5761 | bytes 46088 | tf_op jit(solution)/shard_map/psum | solution.py:111
  786.6 75.0 %all-reduce.16.cloned.1.call-done = bf16[2048,768]{1,0:T(8,128)(2,1)} async-done(((bf16[2048,768]{1,0:T(8,128)(2,1)}), bf16[2048,768]{1,0:T(8,128)(2,1)}) %all-reduce.16.cloned.1.call-update) | async-done | bytes 3145744 | tf_op jit(solution)/shard_map/psum | solution.py:187
  861.6 7.1 convert_add_fusion
  868.7 143.7 %all-reduce.18.cloned.1.call-done = (f32[3,768,192]{1,2,0:T(8,128)}, f32[192,768]{1,0:T(8,128)}, f32[768,768]{1,0:T(8,128)}, f32[768,768]{1,0:T(8,128)}, f32[3,512,512]{1,2,0:T(8,128)}) async-done(((f32[3,768,192]{1,2,0:T(8,128)}, f32[192,768]{1,0:T(8,128)}, f32[768,768]{1,0:T(8,128)}, f32[768,768]{1,0:T(8,128)}, f32[3,512,512]{1,2,0:T(8,128)}), (f32[3,768,192]{1,2,0:T(8,128)}, f32[192,768]{1,0:T(8,128)}, ...) | async-done | bytes 10223632 | tf_op jit(solution)/shard_map/psum | solution.py:191
  1012.4 3.7 copy.66
  (408 shorter events, 112.9 us)
Async XLA Ops:
  7.2 267.7 %copy-start = (bf16[768,768]{1,0:T(8,128)(2,1)S(1)}, bf16[768,768]{1,0:T(8,128)(2,1)}, u32[]{:S(2)}) copy-start(bf16[768,768]{1,0:T(8,128)(2,1)} %param.46) | copy-start | bytes 3538948
  7.2 261.2 %all-reduce.10.cloned.1.call-start = ((), (), s32[]{:S(2)}) async-start(), calls=%async_computation | async-start | bytes 6291456 | tf_op jit(solution)/shard_map/psum | solution.py:98
  19.4 106.7 %copy-start.19 = (bf16[1,2048,192]{1,2,0:T(8,128)(2,1)}, bf16[1,2048,192]{1,2,0:T(8,128)(2,1)S(1)}, u32[]{:S(2)}) copy-start(bf16[1,2048,192]{1,2,0:T(8,128)(2,1)S(1)} %slice.312) | copy-start | bytes 2359300
  26.7 108.1 %copy-start.73 = (f32[3,64]{1,0:T(4,128)}, f32[3,64]{1,0:T(4,128)S(1)}, u32[]{:S(2)}) copy-start(f32[3,64]{1,0:T(4,128)S(1)} %add.308) | copy-start | bytes 2308
  140.8 127.7 %copy-start.61 = (f32[768]{0:T(1024)S(1)}, f32[768]{0:T(1024)}, u32[]{:S(2)}) copy-start(f32[768]{0:T(1024)} %param.43) | copy-start | bytes 9220
  144.5 130.4 %copy-start.75 = (f32[768]{0:T(1024)S(1)}, f32[768]{0:T(1024)}, u32[]{:S(2)}) copy-start(f32[768]{0:T(1024)} %param.44) | copy-start | bytes 9220
  144.5 130.4 %copy-start.107 = (f32[768]{0:T(1024)S(1)}, f32[768]{0:T(1024)}, u32[]{:S(2)}) copy-start(f32[768]{0:T(1024)} %param.45) | copy-start | bytes 9220
  144.5 130.4 %copy-start.118 = (f32[768]{0:T(1024)S(1)}, f32[768]{0:T(1024)}, u32[]{:S(2)}) copy-start(f32[768]{0:T(1024)} %param.47) | copy-start | bytes 9220
  144.5 275.0 %all-reduce.12.cloned.1.call-start = ((), (), s32[]{:S(2)}) async-start(), calls=%async_computation.1 | async-start | bytes 6291456 | tf_op jit(solution)/shard_map/psum | solution.py:105
  274.9 309.0 %copy-start.54 = (f32[2048]{0:T(1024)}, f32[2048]{0:T(1024)S(1)}, u32[]{:S(2)}) copy-start(f32[2048]{0:T(1024)S(1)} %fusion.112) | copy-start | bytes 24580
  274.9 20.4 %copy-start.115 = (bf16[768,768]{1,0:T(8,128)(2,1)S(1)}, bf16[768,768]{1,0:T(8,128)(2,1)}, u32[]{:S(2)}) copy-start(bf16[768,768]{1,0:T(8,128)(2,1)} %param.48) | copy-start | bytes 3538948
  295.3 124.2 %copy-start.105 = (f32[768]{0:T(1024)S(1)}, f32[768]{0:T(1024)}, u32[]{:S(2)}) copy-start(f32[768]{0:T(1024)} %param.49) | copy-start | bytes 9220
  299.3 274.5 %all-reduce.14.cloned.1.call-start = ((), (), s32[]{:S(2)}) async-start(), calls=%async_computation.2 | async-start | bytes 6291456 | tf_op jit(solution)/shard_map/psum | solution.py:124
  437.3 10.6 %copy-start.6 = (f32[2048,768]{1,0:T(8,128)}, f32[2048,768]{1,0:T(8,128)S(1)}, u32[]{:S(2)}) copy-start(f32[2048,768]{1,0:T(8,128)S(1)} %get-tuple-element.208) | copy-start | bytes 18874372
  438.5 9.4 copy-start.30
  453.6 408.0 %all-reduce.16.cloned.1.call-start = ((), (), s32[]{:S(2)}) async-start(), calls=%async_computation.3 | async-start | bytes 6291456 | tf_op jit(solution)/shard_map/psum | solution.py:187
  453.7 142.7 %copy-start.59 = (f32[3,512]{1,0:T(4,128)}, f32[3,512]{1,0:T(4,128)S(1)}, u32[]{:S(2)}) copy-start(f32[3,512]{1,0:T(4,128)S(1)} %log_add_fusion.3) | copy-start | bytes 18436
  454.4 147.1 %copy-start.57 = (f32[3,512]{1,0:T(4,128)}, f32[3,512]{1,0:T(4,128)S(1)}, u32[]{:S(2)}) copy-start(f32[3,512]{1,0:T(4,128)S(1)} %log_add_fusion.2) | copy-start | bytes 18436
  573.8 10.1 copy-start.8
  573.8 10.1 copy-start.11
  573.8 10.1 copy-start.23
  591.6 7.9 copy-start.21
  591.6 7.9 slice-start.12
  604.6 10.9 %copy-start.32 = (bf16[1536,192]{0,1:T(8,128)(2,1)S(1)}, bf16[1536,192]{0,1:T(8,128)(2,1)}, u32[]{:S(2)}) copy-start(bf16[1536,192]{0,1:T(8,128)(2,1)} %slice.289) | copy-start | bytes 1769476
  604.6 10.9 %copy-start.56 = (f32[3,512]{1,0:T(4,128)S(1)}, f32[3,512]{1,0:T(4,128)}, u32[]{:S(2)}) copy-start(f32[3,512]{1,0:T(4,128)} %log_add_fusion.1) | copy-start | bytes 18436
  627.5 7.4 copy-start.74
  634.9 10.8 %slice-start = ((s8[12582912]{0:T(1024)(128)(4,1)}), s8[4194304]{0:T(1024)(128)(4,1)S(1)}, s32[]{:S(2)}) async-start(s8[12582912]{0:T(1024)(128)(4,1)} %bitcast.160), calls=%async_computation.5 | async-start | bytes 8388608
  634.9 10.8 %slice-start.1 = ((s8[12582912]{0:T(1024)(128)(4,1)}), s8[4194304]{0:T(1024)(128)(4,1)S(1)}, s32[]{:S(2)}) async-start(s8[12582912]{0:T(1024)(128)(4,1)} %bitcast.160), calls=%async_computation.6 | async-start | bytes 8388608
  634.9 12.6 %slice-start.2 = ((s8[12582912]{0:T(1024)(128)(4,1)}), s8[4194304]{0:T(1024)(128)(4,1)S(1)}, s32[]{:S(2)}) async-start(s8[12582912]{0:T(1024)(128)(4,1)} %bitcast.160), calls=%async_computation.7 | async-start | bytes 8388608
  647.6 9.0 copy-start.20
  713.5 12.3 %slice-start.14 = ((s8[6291456]{0:T(1024)(128)(4,1)}), s8[4194304]{0:T(1024)(128)(4,1)S(1)}, s32[]{:S(2)}) async-start(s8[6291456]{0:T(1024)(128)(4,1)} %bitcast.170), calls=%async_computation.19 | async-start | bytes 8388608
  713.5 11.1 %copy-start.42 = (bf16[1,512,192]{1,2,0:T(8,128)(2,1)S(1)}, bf16[1,512,192]{1,2,0:T(8,128)(2,1)}, u32[]{:S(2)}) copy-start(bf16[1,512,192]{1,2,0:T(8,128)(2,1)} %slice.285) | copy-start | bytes 589828
  713.5 11.5 %copy-start.41 = (bf16[512,192]{0,1:T(8,128)(2,1)S(1)}, bf16[512,192]{0,1:T(8,128)(2,1)}, u32[]{:S(2)}) copy-start(bf16[512,192]{0,1:T(8,128)(2,1)} %get-tuple-element.221) | copy-start | bytes 589828
  713.5 12.1 %copy-start.45 = (f32[512,3,64]{0,2,1:T(8,128)S(1)}, f32[512,3,64]{0,2,1:T(8,128)}, u32[]{:S(2)}) copy-start(f32[512,3,64]{0,2,1:T(8,128)} %fusion.85) | copy-start | bytes 1179652
  713.5 12.3 %slice-start.15 = ((s8[6291456]{0:T(1024)(128)(4,1)}), s8[2097152]{0:T(1024)(128)(4,1)S(1)}, s32[]{:S(2)}) async-start(s8[6291456]{0:T(1024)(128)(4,1)} %bitcast.170), calls=%async_computation.20 | async-start | bytes 4194304
  713.5 12.3 %copy-start.58 = (f32[3,512]{1,0:T(4,128)S(1)}, f32[3,512]{1,0:T(4,128)}, u32[]{:S(2)}) copy-start(f32[3,512]{1,0:T(4,128)} %copy-done.57) | copy-start | bytes 18436
  713.5 13.6 %slice-start.9 = ((s8[9437184]{0:T(1024)(128)(4,1)}), s8[4194304]{0:T(1024)(128)(4,1)S(1)}, s32[]{:S(2)}) async-start(s8[9437184]{0:T(1024)(128)(4,1)} %bitcast.166), calls=%async_computation.14 | async-start | bytes 8388608
  713.5 13.6 %slice-start.10 = ((s8[9437184]{0:T(1024)(128)(4,1)}), s8[4194304]{0:T(1024)(128)(4,1)S(1)}, s32[]{:S(2)}) async-start(s8[9437184]{0:T(1024)(128)(4,1)} %bitcast.166), calls=%async_computation.15 | async-start | bytes 8388608
  741.4 7.4 copy-start.55
  741.4 7.4 copy-start.62
  741.4 7.4 copy-start.76
  741.4 7.4 copy-start.108
  741.4 271.0 %all-reduce.18.cloned.1.call-start = ((), (), s32[]{:S(2)}) async-start(), calls=%async_computation.4 | async-start | bytes 20447232 | tf_op jit(solution)/shard_map/psum | solution.py:191
  741.7 7.1 copy-start.9
  741.8 7.1 copy-start.12
  758.6 103.0 %copy-start.64 = (f32[2048]{0:T(1024)S(1)}, f32[2048]{0:T(1024)}, u32[]{:S(2)}) copy-start(f32[2048]{0:T(1024)} %copy-done.63) | copy-start | bytes 24580
  1012.4 8.6 copy-start.34
  1016.1 7.7 copy-start.1
  (106 other events, 357.0 us)
Sparse Core Ops, SparseCore 0:
  144.6 123.7 all-reduce.9
  299.4 120.0 all-reduce.11
  453.7 120.0 all-reduce.13
  741.5 120.0 all-reduce.15
  867.0 145.3 all-reduce.17
where the time goes:
time: 1040 us; the launch traced here: 1030 us
  waiting for transfers between devices  566 us (54%)
  local copies, waits for them, and re-layouts  153 us (15%)
  other arithmetic  127 us (12%)
  matrix products  126 us (12%)
  blocking collectives  40.6 us (4%)
  between operations  19.2 us (2%)
    psum x1, waiting for transfers between devices, body(): lax.psum((grad_w_qkv, grad_b_qv, grad_w_attn_out, grad_b_attn_out, grad_g...  144 us
    psum x1, waiting for transfers between devices, body(): lax.psum(attn_part.astype(jnp.bfloat16), 'tensor').astype(jnp.float32)  124 us
    psum x1, waiting for transfers between devices, body(): lax.psum(back_first.astype(jnp.bfloat16), 'tensor').astype(jnp.float32)  119 us
    psum x1, waiting for transfers between devices, body(): lax.psum(ffn_part.astype(jnp.bfloat16), 'tensor').astype(jnp.float32)  104 us
    psum x1, waiting for transfers between devices, body(): lax.psum(back_hidden.astype(jnp.bfloat16), 'tensor').astype(jnp.float32)  75 us
    another operation x6, local copies, waits for them, and re-layouts, block_scores(): scores = scores + jnp.tile(gate_natural_log, (1, 1, block_index + 1))  56 us
    unnamed x305, local copies, waits for them, and re-layouts  45.1 us
    psum x2, blocking collectives, body(): total_valid, total_error = lax.psum((local_count, local_error), 'dp')  40.6 us
  transfers between devices with their start and end apart: 5, of which 5 were waited for; matrix products, arithmetic and copies ran while one was open for 2% of the time, Pallas kernels for 0%

commit v1 on v0

--- a/solution.py
+++ b/solution.py
@@ -102,7 +102,10 @@
     activated, gelu_pull = jax.vjp(exact_gelu, before)
     act_low = activated.astype(jnp.bfloat16)
     ffn_part = jnp.dot(act_low, w_down, preferred_element_type=jnp.float32)
-    feedforward = lax.psum(ffn_part.astype(jnp.bfloat16), "tensor").astype(jnp.float32) + b_down
+    feedforward = (
+        jnp.sum(lax.all_gather(ffn_part.astype(jnp.bfloat16), "tensor"), axis=0).astype(jnp.float32)
+        + b_down
+    )
     out_states, second_pull = jax.vjp(normed, first + feedforward, gain_two, bias_two)
     valid_rows = valid[0].astype(jnp.float32)[:, None]
     residue = out_states - teacher

time: 1040 us -> 1150 us (1.11)
  waiting for transfers between devices: 566 us -> 663 us
    all_gather x0 -> x1, waiting for transfers between devices: none -> 202 us  [body(): lax.all_gather(ffn_part.astype(jnp.bfloat16), 'tensor')]
    psum x1 -> x0, waiting for transfers between devices: 104 us -> none  [body(): lax.psum(ffn_part.astype(jnp.bfloat16), 'tensor').astype(jnp.float32)]
where the time goes in v1:
time: 1150 us; the launch traced here: 1140 us
  waiting for transfers between devices  663 us (58%)
  local copies, waits for them, and re-layouts  153 us (13%)
  other arithmetic  136 us (12%)
  matrix products  126 us (11%)
  blocking collectives  40.2 us (3%)
  between operations  19.2 us (2%)
    all_gather x1, waiting for transfers between devices, body(): lax.all_gather(ffn_part.astype(jnp.bfloat16), 'tensor')  202 us
    psum x1, waiting for transfers between devices, body(): lax.psum((grad_w_qkv, grad_b_qv, grad_w_attn_out, grad_b_attn_out, grad_g...  144 us
    psum x1, waiting for transfers between devices, body(): lax.psum(attn_part.astype(jnp.bfloat16), 'tensor').astype(jnp.float32)  124 us
    psum x1, waiting for transfers between devices, body(): lax.psum(back_first.astype(jnp.bfloat16), 'tensor').astype(jnp.float32)  119 us
    psum x1, waiting for transfers between devices, body(): lax.psum(back_hidden.astype(jnp.bfloat16), 'tensor').astype(jnp.float32)  75 us
    another operation x6, local copies, waits for them, and re-layouts, block_scores(): scores = scores + jnp.tile(gate_natural_log, (1, 1, block_index + 1))  56 us
    unnamed x305, local copies, waits for them, and re-layouts  45.2 us
    psum x2, blocking collectives, body(): total_valid, total_error = lax.psum((local_count, local_error), 'dp')  40.2 us
  transfers between devices with their start and end apart: 5, of which 5 were waited for; matrix products, arithmetic and copies ran while one was open for 2% of the time, Pallas kernels for 0%

profile of v1, /device:TPU:0, one launch (start us, length us, event | category | flops | bytes accessed | tf_op | source)
XLA Modules:
  0.0 1137.1 jit_solution(2344270272187298622)
XLA Ops:
  15.1 4.2 convolution_bitcast_fusion
  26.7 3.5 copy.54
  30.2 3.6 copy.55
  33.8 6.4 fusion.35
  40.2 3.6 copy.57
  46.0 7.0 tile.14
  53.0 9.6 copy.58
  62.6 6.6 tile.12
  69.1 9.2 tile.13
  78.3 7.7 tile.16
  86.1 15.9 %tile.17 = f32[3,512,2048]{2,1,0:T(8,128)} reshape(f32[3,512,4,512]{3,2,1,0:T(4,128)} %tile.16) | data formatting | bytes 25165824 | tf_op jit(solution)/shard_map/tile | solution.py:34
  126.1 6.7 fusion.143
  137.5 3.2 fusion.97
  144.6 123.8 %all-reduce.9.cloned.1.call-done = bf16[2048,768]{1,0:T(8,128)(2,1)} async-done(((bf16[2048,768]{1,0:T(8,128)(2,1)}), bf16[2048,768]{1,0:T(8,128)(2,1)}) %all-reduce.9.cloned.1.call-update) | async-done | bytes 3145744 | tf_op jit(solution)/shard_map/psum | solution.py:98
  268.4 4.1 fusion.17
  274.9 18.6 %multiply_convert_fusion.3 = (bf16[2048,768]{1,0:T(8,128)(2,1)S(1)}, f32[2048,768]{1,0:T(8,128)}, f32[2048,768]{1,0:T(8,128)}) fusion(f32[768]{0:T(1024)S(1)} %copy-done.118, bf16[768,768]{1,0:T(8,128)(2,1)S(1)} %copy-done, f32[768]{0:T(1024)S(1)} %copy-done.107, f32[768]{0:T(1024)S(1)} %copy-done.75, f32[2048]{0:T(1024)S(1)} %fusion.112, ...), kind=kOutput, calls=%fused_computation.44 | convolution fusion | flops 2533883904 | bytes 23228416 | tf_op jit(solution)/shard_map/dot_general | solution.py:101
  295.3 3.9 convolution_convert_fusion.1
  300.0 14.2 %psum.128 = f32[]{:T(128)} all-reduce(f32[]{:T(128)} %convert_reduce_fusion.4), channel_id=1, replica_groups=mesh['dp'=8,'tensor'=4] {'dp'}, use_global_device_ids=true, to_apply=%region_17.18 | all-reduce | flops 1 | bytes 8 | tf_op jit(solution)/shard_map/psum | solution.py:114
  314.9 201.7 %all-gather.3.cloned.1.call-done = bf16[8192,768]{1,0:T(8,128)(2,1)} async-done(((bf16[2048,768]{1,0:T(8,128)(2,1)}), bf16[8192,768]{1,0:T(8,128)(2,1)}) %all-gather.3.cloned.1.call-update) | async-done | bytes 12582928 | tf_op jit(solution)/shard_map/all_gather | solution.py:106
  516.7 9.0 reduce_sum.315
  525.6 5.2 fusion.138
  531.8 8.2 multiply_reduce_fusion.2
  540.0 3.4 fusion.137
  545.5 8.4 convert_reduce_fusion.1
  555.6 4.0 convolution_convert_fusion
  560.5 118.6 %all-reduce.11.cloned.1.call-done = bf16[2048,768]{1,0:T(8,128)(2,1)} async-done(((bf16[2048,768]{1,0:T(8,128)(2,1)}), bf16[2048,768]{1,0:T(8,128)(2,1)}) %all-reduce.11.cloned.1.call-update) | async-done | bytes 3145744 | tf_op jit(solution)/shard_map/psum | solution.py:127
  679.1 10.1 multiply_reduce_fusion.3
  689.2 6.0 fusion.136
  711.6 9.1 reshape.827
  720.7 5.2 multiply_reduce_fusion.1
  732.8 7.4 copy.64
  740.2 10.8 multiply_reduce_fusion
  752.8 6.3 multiply_convert_fusion
  764.6 15.4 %reshape.829 = f32[3,512,4,512]{3,2,1,0:T(4,128)} reshape(bf16[3,512,2048]{2,1,0:T(8,128)(2,1)} %copy-done.5) | data formatting | bytes 18874368 | tf_op jit(solution)/shard_map/convert_element_type | solution.py:157
  780.0 11.9 %reduce_sum.336 = f32[3,512,512]{2,1,0:T(8,128)} reduce(f32[3,512,2,512]{3,2,1,0:T(2,128)} %reshape.827, f32[]{:T(128)} %constant.387.clone.1), dimensions={2}, to_apply=%region_48.49 | reduce | flops 786432 | bytes 9437188 | tf_op jit(solution)/shard_map/reduce_sum | solution.py:157
  791.8 3.5 copy.63
  795.4 7.0 reduce_sum.337
  802.4 12.7 %reduce_sum.338 = f32[3,512,512]{2,1,0:T(8,128)} reduce(f32[3,512,4,512]{3,2,1,0:T(4,128)} %reshape.829, f32[]{:T(128)} %constant.387.clone.1), dimensions={2}, to_apply=%region_50.51 | reduce | flops 2359296 | bytes 15728644 | tf_op jit(solution)/shard_map/reduce_sum | solution.py:157
  815.0 3.7 copy.65
  818.8 11.1 fusion.30
  842.6 4.1 bitcast_convert_fusion
  847.0 7.1 fusion.148
  854.2 4.8 fusion.129
  865.2 26.0 %all-reduce.2 = (f32[]{:T(128)}, f32[2,192]{1,0:T(2,128)}, f32[768]{0:T(1024)}, f32[768]{0:T(1024)}, f32[768]{0:T(1024)}, /*index=5*/f32[768]{0:T(1024)}, f32[768]{0:T(1024)}, f32[768]{0:T(1024)}, f32[768]{0:T(1024)}) all-reduce(f32[]{:T(128)} %get-tuple-element.182, ...), channel_id=1, replica_groups=mesh['dp'=8,'tensor'=4] {'dp'}, use_global_device_ids=true, to_apply=%region_15.16 | all-reduce | flops 5761 | bytes 46088 | tf_op jit(solution)/shard_map/psum | solution.py:114
  891.9 75.0 %all-reduce.13.cloned.1.call-done = bf16[2048,768]{1,0:T(8,128)(2,1)} async-done(((bf16[2048,768]{1,0:T(8,128)(2,1)}), bf16[2048,768]{1,0:T(8,128)(2,1)}) %all-reduce.13.cloned.1.call-update) | async-done | bytes 3145744 | tf_op jit(solution)/shard_map/psum | solution.py:190
  966.9 7.1 convert_add_fusion
  974.0 143.7 %all-reduce.15.cloned.1.call-done = (f32[3,768,192]{1,2,0:T(8,128)}, f32[192,768]{1,0:T(8,128)}, f32[768,768]{1,0:T(8,128)}, f32[768,768]{1,0:T(8,128)}, f32[3,512,512]{1,2,0:T(8,128)}) async-done(((f32[3,768,192]{1,2,0:T(8,128)}, f32[192,768]{1,0:T(8,128)}, f32[768,768]{1,0:T(8,128)}, f32[768,768]{1,0:T(8,128)}, f32[3,512,512]{1,2,0:T(8,128)}), (f32[3,768,192]{1,2,0:T(8,128)}, f32[192,768]{1,0:T(8,128)}, ...) | async-done | bytes 10223632 | tf_op jit(solution)/shard_map/psum | solution.py:194
  1117.7 3.7 copy.66
  (409 shorter events, 116.1 us)
Async XLA Ops:
  7.2 267.7 %copy-start = (bf16[768,768]{1,0:T(8,128)(2,1)S(1)}, bf16[768,768]{1,0:T(8,128)(2,1)}, u32[]{:S(2)}) copy-start(bf16[768,768]{1,0:T(8,128)(2,1)} %param.46) | copy-start | bytes 3538948
  7.2 261.2 %all-reduce.9.cloned.1.call-start = ((), (), s32[]{:S(2)}) async-start(), calls=%async_computation | async-start | bytes 6291456 | tf_op jit(solution)/shard_map/psum | solution.py:98
  19.4 106.7 %copy-start.19 = (bf16[1,2048,192]{1,2,0:T(8,128)(2,1)}, bf16[1,2048,192]{1,2,0:T(8,128)(2,1)S(1)}, u32[]{:S(2)}) copy-start(bf16[1,2048,192]{1,2,0:T(8,128)(2,1)S(1)} %slice.312) | copy-start | bytes 2359300
  26.7 108.1 %copy-start.73 = (f32[3,64]{1,0:T(4,128)}, f32[3,64]{1,0:T(4,128)S(1)}, u32[]{:S(2)}) copy-start(f32[3,64]{1,0:T(4,128)S(1)} %add.306) | copy-start | bytes 2308
  140.8 127.7 %copy-start.61 = (f32[768]{0:T(1024)S(1)}, f32[768]{0:T(1024)}, u32[]{:S(2)}) copy-start(f32[768]{0:T(1024)} %param.43) | copy-start | bytes 9220
  144.5 130.4 %copy-start.75 = (f32[768]{0:T(1024)S(1)}, f32[768]{0:T(1024)}, u32[]{:S(2)}) copy-start(f32[768]{0:T(1024)} %param.44) | copy-start | bytes 9220
  144.5 130.4 %copy-start.107 = (f32[768]{0:T(1024)S(1)}, f32[768]{0:T(1024)}, u32[]{:S(2)}) copy-start(f32[768]{0:T(1024)} %param.45) | copy-start | bytes 9220
  144.5 130.4 %copy-start.118 = (f32[768]{0:T(1024)S(1)}, f32[768]{0:T(1024)}, u32[]{:S(2)}) copy-start(f32[768]{0:T(1024)} %param.47) | copy-start | bytes 9220
  144.5 372.1 %all-gather.3.cloned.1.call-start = ((), (), s32[]{:S(2)}) async-start(), calls=%async_computation.3 | async-start | bytes 15728640 | tf_op jit(solution)/shard_map/all_gather | solution.py:106
  274.9 414.3 %copy-start.54 = (f32[2048]{0:T(1024)}, f32[2048]{0:T(1024)S(1)}, u32[]{:S(2)}) copy-start(f32[2048]{0:T(1024)S(1)} %fusion.112) | copy-start | bytes 24580
  274.9 20.4 %copy-start.115 = (bf16[768,768]{1,0:T(8,128)(2,1)S(1)}, bf16[768,768]{1,0:T(8,128)(2,1)}, u32[]{:S(2)}) copy-start(bf16[768,768]{1,0:T(8,128)(2,1)} %param.48) | copy-start | bytes 3538948
  299.3 379.8 %all-reduce.11.cloned.1.call-start = ((), (), s32[]{:S(2)}) async-start(), calls=%async_computation.1 | async-start | bytes 6291456 | tf_op jit(solution)/shard_map/psum | solution.py:127
  516.6 9.0 copy-start.105
  543.4 10.6 copy-start.6
  544.6 9.4 copy-start.30
  559.7 407.2 %all-reduce.13.cloned.1.call-start = ((), (), s32[]{:S(2)}) async-start(), calls=%async_computation.2 | async-start | bytes 6291456 | tf_op jit(solution)/shard_map/psum | solution.py:190
  559.8 141.9 %copy-start.59 = (f32[3,512]{1,0:T(4,128)}, f32[3,512]{1,0:T(4,128)S(1)}, u32[]{:S(2)}) copy-start(f32[3,512]{1,0:T(4,128)S(1)} %log_add_fusion.3) | copy-start | bytes 18436
  560.4 146.3 %copy-start.57 = (f32[3,512]{1,0:T(4,128)}, f32[3,512]{1,0:T(4,128)S(1)}, u32[]{:S(2)}) copy-start(f32[3,512]{1,0:T(4,128)S(1)} %log_add_fusion.2) | copy-start | bytes 18436
  679.1 10.1 copy-start.8
  679.1 10.1 copy-start.11
  679.1 10.1 copy-start.23
  696.9 7.9 copy-start.21
  696.9 7.9 slice-start.12
  709.8 10.9 copy-start.32
  709.8 10.9 copy-start.56
  732.8 7.4 copy-start.74
  740.2 10.8 slice-start
  740.2 10.8 slice-start.1
  740.2 12.6 %slice-start.2 = ((s8[12582912]{0:T(1024)(128)(4,1)}), s8[4194304]{0:T(1024)(128)(4,1)S(1)}, s32[]{:S(2)}) async-start(s8[12582912]{0:T(1024)(128)(4,1)} %bitcast.161), calls=%async_computation.7 | async-start | bytes 8388608
  752.8 9.0 copy-start.20
  818.7 12.3 %slice-start.14 = ((s8[6291456]{0:T(1024)(128)(4,1)}), s8[4194304]{0:T(1024)(128)(4,1)S(1)}, s32[]{:S(2)}) async-start(s8[6291456]{0:T(1024)(128)(4,1)} %bitcast.171), calls=%async_computation.19 | async-start | bytes 8388608
  818.7 11.1 copy-start.42
  818.7 11.5 %copy-start.41 = (bf16[512,192]{0,1:T(8,128)(2,1)S(1)}, bf16[512,192]{0,1:T(8,128)(2,1)}, u32[]{:S(2)}) copy-start(bf16[512,192]{0,1:T(8,128)(2,1)} %get-tuple-element.221) | copy-start | bytes 589828
  818.8 12.1 %copy-start.45 = (f32[512,3,64]{0,2,1:T(8,128)S(1)}, f32[512,3,64]{0,2,1:T(8,128)}, u32[]{:S(2)}) copy-start(f32[512,3,64]{0,2,1:T(8,128)} %fusion.85) | copy-start | bytes 1179652
  818.8 12.3 %slice-start.15 = ((s8[6291456]{0:T(1024)(128)(4,1)}), s8[2097152]{0:T(1024)(128)(4,1)S(1)}, s32[]{:S(2)}) async-start(s8[6291456]{0:T(1024)(128)(4,1)} %bitcast.171), calls=%async_computation.20 | async-start | bytes 4194304
  818.8 12.3 %copy-start.58 = (f32[3,512]{1,0:T(4,128)S(1)}, f32[3,512]{1,0:T(4,128)}, u32[]{:S(2)}) copy-start(f32[3,512]{1,0:T(4,128)} %copy-done.57) | copy-start | bytes 18436
  818.8 13.6 %slice-start.9 = ((s8[9437184]{0:T(1024)(128)(4,1)}), s8[4194304]{0:T(1024)(128)(4,1)S(1)}, s32[]{:S(2)}) async-start(s8[9437184]{0:T(1024)(128)(4,1)} %bitcast.167), calls=%async_computation.14 | async-start | bytes 8388608
  818.8 13.6 %slice-start.10 = ((s8[9437184]{0:T(1024)(128)(4,1)}), s8[4194304]{0:T(1024)(128)(4,1)S(1)}, s32[]{:S(2)}) async-start(s8[9437184]{0:T(1024)(128)(4,1)} %bitcast.167), calls=%async_computation.15 | async-start | bytes 8388608
  846.7 7.4 copy-start.55
  846.7 7.4 copy-start.62
  846.7 7.4 copy-start.76
  846.7 7.4 copy-start.108
  846.7 270.9 %all-reduce.15.cloned.1.call-start = ((), (), s32[]{:S(2)}) async-start(), calls=%async_computation.4 | async-start | bytes 20447232 | tf_op jit(solution)/shard_map/psum | solution.py:194
  847.0 7.1 copy-start.9
  847.0 7.1 copy-start.12
  863.9 103.0 %copy-start.64 = (f32[2048]{0:T(1024)S(1)}, f32[2048]{0:T(1024)}, u32[]{:S(2)}) copy-start(f32[2048]{0:T(1024)} %copy-done.63) | copy-start | bytes 24580
  1117.7 8.6 copy-start.34
  1121.4 7.7 copy-start.1
  (106 other events, 356.9 us)
Sparse Core Ops, SparseCore 0:
  144.6 123.7 all-reduce.8
  299.4 217.1 all-gather.2
  559.8 119.2 all-reduce.10
  846.8 120.0 all-reduce.12
  972.3 145.3 all-reduce.14
